TPU v7x, 256 devices: a whole 4x4x8 slice. The times are simulated.
256 devices in a mesh: rows: 16 (over x, z_hi, core), params: 16 (over z_lo, y).
Axes of the slice: x: 4, y: 4, z: 8 (z_hi: 2, z_lo: 4; z = z_hi * 4 + z_lo), core: 2. Of those that a mesh axis runs over, the one named last changes fastest.
Arguments:
- jacobian: bfloat16 [32768, 12288], P('rows', 'params'), may hold values from -0.0546875 to 0.0546875
- pattern: int32 [256, 96], P('rows', 'params'), may hold values from 0 to 1, as said below
- row_class: int32 [32768], P('rows'), may hold values from 0 to 15
- class_weight: float32 [16], replicated, may hold values from 0.1 to 10
- probes: bfloat16 [32, 12288], P(None, 'params'), may hold values from -6 to 6
Outputs:
- basis: bfloat16 [32, 12288], P(None, 'params')
Inputs may be any that keep to these rules, and one draw needn't show every extreme that they name: `pattern`: 1 marks a nonzero block of the Jacobian, 0 a zero block.
All inputs are finite; a program needn't handle non-finite values.
Results may differ from a plain program's by a relative error of at most 0.0075.
Values may be sent and summed in bfloat16 or wider, within the bound.
A program may use at most 64 MiB of HBM per device.

v0:
```python
import math
import jax
import jax.numpy as jnp
from jax import lax
from jax.sharding import PartitionSpec as P

P_SIZE = 12288
ITERS = 4


def local(jacobian, pattern, row_class, class_weight, probes):
    block = jacobian.shape[0] // pattern.shape[0]
    mask_full = jnp.repeat(jnp.repeat(pattern, block, axis=0), block, axis=1)
    masked = jacobian * mask_full.astype(jnp.bfloat16)
    classes = jnp.arange(class_weight.shape[0], dtype=jnp.int32)
    onehot = (row_class[None, :] == classes[:, None]).astype(jnp.float32)
    weight = jnp.sum(onehot * class_weight[:, None], axis=0)
    scale = math.sqrt(P_SIZE)
    basis = probes
    for step in range(ITERS):
        zpart = lax.dot_general(
            basis, masked, (((1,), (1,)), ((), ())), preferred_element_type=jnp.float32
        )
        ztotal = lax.psum(zpart, "params")
        weighted = (ztotal * weight[None, :]).astype(jnp.bfloat16)
        ypart = jnp.dot(weighted, masked, preferred_element_type=jnp.float32)
        ytotal = lax.psum(ypart, "rows")
        gram = lax.psum(jnp.dot(ytotal, ytotal.T, precision=lax.Precision.HIGHEST), "params")
        lower = jnp.linalg.cholesky(gram)
        solved = lax.linalg.triangular_solve(lower, ytotal, left_side=True, lower=True)
        basis = (solved * scale).astype(jnp.bfloat16)
    return basis


def solution(mesh):
    placed = (P("rows", "params"), P("rows", "params"), P("rows"), P(), P(None, "params"))
    return jax.shard_map(
        local, mesh=mesh, in_specs=placed, out_specs=P(None, "params"), check_vma=False
    )
```

profile of v0, /device:TPU:0, one launch (start us, length us, event | category | flops | bytes accessed | tf_op | source)
XLA Modules:
  0.0 1694.4 jit_solution(16454283900543719052)
XLA Ops:
  6.5 0.7 convert_element_type.36
  7.3 4.8 copy.24
  12.1 2.1 bitcast_multiply_fusion
  14.3 1.4 convolution_bitcast_fusion
  15.7 0.1 select_reduce_fusion
  15.8 162.7 %all-reduce.9.cloned.1.call-done = f32[32,2048]{1,0:T(8,128)} async-done(((f32[32,2048]{1,0:T(8,128)}), f32[32,2048]{1,0:T(8,128)}) %all-reduce.9.cloned.1.call-update) | async-done | bytes 262160 | tf_op jit(solution)/shard_map/psum | solution.py:24
  178.5 2.6 fusion.4
  181.2 170.3 %all-reduce.11.cloned.1.call-done = f32[32,768]{1,0:T(8,128)} async-done(((f32[32,768]{1,0:T(8,128)}), f32[32,768]{1,0:T(8,128)}) %all-reduce.11.cloned.1.call-update) | async-done | bytes 98320 | tf_op jit(solution)/shard_map/psum | solution.py:27
  351.5 1.2 fusion.30
  352.7 79.5 %psum.86 = f32[32,32]{0,1:T(8,128)S(1)} all-reduce(f32[32,32]{0,1:T(8,128)S(1)} %fusion.30), channel_id=1, replica_groups=mesh['rows'=16,'params'=16] {'params'}, use_global_device_ids=true, to_apply=%region_3.0 | all-reduce | flops 1024 | bytes 8192 | tf_op jit(solution)/shard_map/psum | solution.py:28
  432.4 2.9 cholesky.74
  435.3 0.6 compare_reduce_fusion.3
  436.0 0.7 fusion.12
  436.6 2.5 custom-call.8
  439.1 1.2 fusion
  440.3 1.4 fusion.31
  441.7 152.4 %all-reduce.13.cloned.1.call-done = f32[32,2048]{1,0:T(8,128)} async-done(((f32[32,2048]{1,0:T(8,128)}), f32[32,2048]{1,0:T(8,128)}) %all-reduce.13.cloned.1.call-update) | async-done | bytes 262160 | tf_op jit(solution)/shard_map/psum | solution.py:24
  594.1 2.6 fusion.5
  596.8 170.3 %all-reduce.15.cloned.1.call-done = f32[32,768]{1,0:T(8,128)} async-done(((f32[32,768]{1,0:T(8,128)}), f32[32,768]{1,0:T(8,128)}) %all-reduce.15.cloned.1.call-update) | async-done | bytes 98320 | tf_op jit(solution)/shard_map/psum | solution.py:27
  767.1 1.2 fusion.32
  768.3 79.5 %psum.89 = f32[32,32]{0,1:T(8,128)S(1)} all-reduce(f32[32,32]{0,1:T(8,128)S(1)} %fusion.32), channel_id=1, replica_groups=mesh['rows'=16,'params'=16] {'params'}, use_global_device_ids=true, to_apply=%region_8.11 | all-reduce | flops 1024 | bytes 8192 | tf_op jit(solution)/shard_map/psum | solution.py:28
  847.9 2.9 cholesky.85
  850.9 0.6 compare_reduce_fusion.2
  851.5 0.7 fusion.13
  852.2 2.5 custom-call.9
  854.6 1.2 fusion.1
  855.8 1.4 fusion.33
  857.2 152.4 %all-reduce.17.cloned.1.call-done = f32[32,2048]{1,0:T(8,128)} async-done(((f32[32,2048]{1,0:T(8,128)}), f32[32,2048]{1,0:T(8,128)}) %all-reduce.17.cloned.1.call-update) | async-done | bytes 262160 | tf_op jit(solution)/shard_map/psum | solution.py:24
  1009.6 2.6 fusion.6
  1012.3 170.4 %all-reduce.19.cloned.1.call-done = f32[32,768]{1,0:T(8,128)} async-done(((f32[32,768]{1,0:T(8,128)}), f32[32,768]{1,0:T(8,128)}) %all-reduce.19.cloned.1.call-update) | async-done | bytes 98320 | tf_op jit(solution)/shard_map/psum | solution.py:27
  1182.6 1.2 fusion.34
  1183.8 79.5 %psum.92 = f32[32,32]{0,1:T(8,128)S(1)} all-reduce(f32[32,32]{0,1:T(8,128)S(1)} %fusion.34), channel_id=1, replica_groups=mesh['rows'=16,'params'=16] {'params'}, use_global_device_ids=true, to_apply=%region_11.14 | all-reduce | flops 1024 | bytes 8192 | tf_op jit(solution)/shard_map/psum | solution.py:28
  1263.5 2.9 cholesky.96
  1266.4 0.6 compare_reduce_fusion.1
  1267.1 0.7 fusion.14
  1267.7 2.5 custom-call.10
  1270.2 1.2 fusion.2
  1271.4 1.4 fusion.35
  1272.8 152.4 %all-reduce.21.cloned.1.call-done = f32[32,2048]{1,0:T(8,128)} async-done(((f32[32,2048]{1,0:T(8,128)}), f32[32,2048]{1,0:T(8,128)}) %all-reduce.21.cloned.1.call-update) | async-done | bytes 262160 | tf_op jit(solution)/shard_map/psum | solution.py:24
  1425.1 2.6 fusion.7
  1427.8 170.4 %all-reduce.23.cloned.1.call-done = f32[32,768]{1,0:T(8,128)} async-done(((f32[32,768]{1,0:T(8,128)}), f32[32,768]{1,0:T(8,128)}) %all-reduce.23.cloned.1.call-update) | async-done | bytes 98320 | tf_op jit(solution)/shard_map/psum | solution.py:27
  1598.2 1.2 fusion.36
  1599.4 79.5 %psum.95 = f32[32,32]{0,1:T(8,128)S(1)} all-reduce(f32[32,32]{0,1:T(8,128)S(1)} %fusion.36), channel_id=1, replica_groups=mesh['rows'=16,'params'=16] {'params'}, use_global_device_ids=true, to_apply=%region_14.17 | all-reduce | flops 1024 | bytes 8192 | tf_op jit(solution)/shard_map/psum | solution.py:28
  1679.0 2.9 cholesky.107
  1681.9 0.6 compare_reduce_fusion
  1682.6 0.7 fusion.15
  1683.3 2.4 custom-call.11
  1685.7 1.8 fusion.3
  (36 shorter events, 0.9 us)
Async XLA Ops:
  6.5 7.7 copy-start
  6.5 172.0 %all-reduce.9.cloned.1.call-start = ((), (), s32[]{:S(2)}) async-start(), calls=%async_computation | async-start | bytes 524288 | tf_op jit(solution)/shard_map/psum | solution.py:24
  14.2 1.5 copy-start.1
  14.2 1.4 copy-start.2
  15.6 335.9 %all-reduce.11.cloned.1.call-start = ((), (), s32[]{:S(2)}) async-start(), calls=%async_computation.1 | async-start | bytes 196608 | tf_op jit(solution)/shard_map/psum | solution.py:27
  181.2 412.9 %all-reduce.13.cloned.1.call-start = ((), (), s32[]{:S(2)}) async-start(), calls=%async_computation.2 | async-start | bytes 524288 | tf_op jit(solution)/shard_map/psum | solution.py:24
  441.7 325.4 %all-reduce.15.cloned.1.call-start = ((), (), s32[]{:S(2)}) async-start(), calls=%async_computation.3 | async-start | bytes 196608 | tf_op jit(solution)/shard_map/psum | solution.py:27
  596.7 412.9 %all-reduce.17.cloned.1.call-start = ((), (), s32[]{:S(2)}) async-start(), calls=%async_computation.4 | async-start | bytes 524288 | tf_op jit(solution)/shard_map/psum | solution.py:24
  857.2 325.5 %all-reduce.19.cloned.1.call-start = ((), (), s32[]{:S(2)}) async-start(), calls=%async_computation.5 | async-start | bytes 196608 | tf_op jit(solution)/shard_map/psum | solution.py:27
  1012.2 412.9 %all-reduce.21.cloned.1.call-start = ((), (), s32[]{:S(2)}) async-start(), calls=%async_computation.6 | async-start | bytes 524288 | tf_op jit(solution)/shard_map/psum | solution.py:24
  1272.7 325.4 %all-reduce.23.cloned.1.call-start = ((), (), s32[]{:S(2)}) async-start(), calls=%async_computation.7 | async-start | bytes 196608 | tf_op jit(solution)/shard_map/psum | solution.py:27
Sparse Core Ops, SparseCore 0:
  15.8 162.7 all-reduce.8
  181.3 170.2 all-reduce.10
  441.8 152.2 all-reduce.12
  596.8 170.2 all-reduce.14
  857.3 152.2 all-reduce.16
  1012.4 170.2 all-reduce.18
  1272.9 152.2 all-reduce.20
  1427.9 170.2 all-reduce.22
where the time goes:
time: 1700 us; the launch traced here: 1690 us
  waiting for transfers between devices  1300 us (76%)
  blocking collectives  318 us (19%)
  other arithmetic  29.7 us (2%)
  matrix products  26 us (2%)
    psum x4, waiting for transfers between devices, local(): ytotal = lax.psum(ypart, 'rows')  681 us
    psum x4, waiting for transfers between devices, local(): ztotal = lax.psum(zpart, 'params')  620 us
    psum x4, blocking collectives, local(): lax.psum(jnp.dot(ytotal, ytotal.T, precision=lax.Precision.HIGHEST), 'par...  318 us
  transfers between devices with their start and end apart: 8, of which 8 were waited for; matrix products, arithmetic and copies ran while one was open for 0% of the time, Pallas kernels for 0%

commit v1 on v0

--- a/solution.py
+++ b/solution.py
@@ -21,7 +21,7 @@
         zpart = lax.dot_general(
             basis, masked, (((1,), (1,)), ((), ())), preferred_element_type=jnp.float32
         )
-        ztotal = lax.psum(zpart, "params")
+        ztotal = jnp.sum(lax.all_gather(zpart, "params"), axis=0)
         weighted = (ztotal * weight[None, :]).astype(jnp.bfloat16)
         ypart = jnp.dot(weighted, masked, preferred_element_type=jnp.float32)
         ytotal = lax.psum(ypart, "rows")

time: 1700 us -> 1410 us (0.83)
  waiting for transfers between devices: 1300 us -> 1010 us
    psum x4 -> x0, waiting for transfers between devices: 620 us -> none  [local(): ztotal = lax.psum(zpart, 'params')]
    all_gather x0 -> x4, waiting for transfers between devices: none -> 322 us  [local(): ztotal = jnp.sum(lax.all_gather(zpart, 'params'), axis=0)]
where the time goes in v1:
time: 1410 us; the launch traced here: 1400 us
  waiting for transfers between devices  1010 us (72%)
  blocking collectives  318 us (23%)
  other arithmetic  39.4 us (3%)
  matrix products  22.2 us (2%)
    psum x4, waiting for transfers between devices, local(): ytotal = lax.psum(ypart, 'rows')  684 us
    all_gather x4, waiting for transfers between devices, local(): ztotal = jnp.sum(lax.all_gather(zpart, 'params'), axis=0)  322 us
    psum x4, blocking collectives, local(): lax.psum(jnp.dot(ytotal, ytotal.T, precision=lax.Precision.HIGHEST), 'par...  318 us
  transfers between devices with their start and end apart: 8, of which 8 were waited for; matrix products, arithmetic and copies ran while one was open for 0% of the time, Pallas kernels for 0%

profile of v1, /device:TPU:0, one launch (start us, length us, event | category | flops | bytes accessed | tf_op | source)
XLA Modules:
  0.0 1404.3 jit_solution(12945017588949257692)
XLA Ops:
  6.5 0.7 convert_element_type.36
  7.3 4.8 copy.24
  12.1 2.1 bitcast_multiply_fusion
  14.3 1.3 convolution_bitcast_fusion
  15.8 88.2 %all-gather.9.cloned.1.call-done = f32[512,2048]{1,0:T(8,128)} async-done(((f32[32,2048]{1,0:T(8,128)}), f32[512,2048]{1,0:T(8,128)}) %all-gather.9.cloned.1.call-update) | async-done | bytes 4194320 | tf_op jit(solution)/shard_map/all_gather | solution.py:24
  104.0 2.4 reduce_sum.45
  106.4 1.7 fusion.4
  108.1 170.9 %all-reduce.5.cloned.1.call-done = f32[32,768]{1,0:T(8,128)} async-done(((f32[32,768]{1,0:T(8,128)}), f32[32,768]{1,0:T(8,128)}) %all-reduce.5.cloned.1.call-update) | async-done | bytes 98320 | tf_op jit(solution)/shard_map/psum | solution.py:27
  279.0 1.2 fusion.30
  280.2 79.5 %psum.57 = f32[32,32]{0,1:T(8,128)S(1)} all-reduce(f32[32,32]{0,1:T(8,128)S(1)} %fusion.30), channel_id=1, replica_groups=mesh['rows'=16,'params'=16] {'params'}, use_global_device_ids=true, to_apply=%region_3.0 | all-reduce | flops 1024 | bytes 8192 | tf_op jit(solution)/shard_map/psum | solution.py:28
  359.9 2.9 cholesky.74
  363.5 0.7 fusion.12
  364.1 2.5 custom-call.8
  366.6 1.2 fusion
  367.8 1.3 fusion.31
  369.2 77.8 %all-gather.11.cloned.1.call-done = f32[512,2048]{1,0:T(8,128)} async-done(((f32[32,2048]{1,0:T(8,128)}), f32[512,2048]{1,0:T(8,128)}) %all-gather.11.cloned.1.call-update) | async-done | bytes 4194320 | tf_op jit(solution)/shard_map/all_gather | solution.py:24
  447.0 2.4 reduce_sum.47
  449.4 1.7 fusion.5
  451.2 170.9 %all-reduce.7.cloned.1.call-done = f32[32,768]{1,0:T(8,128)} async-done(((f32[32,768]{1,0:T(8,128)}), f32[32,768]{1,0:T(8,128)}) %all-reduce.7.cloned.1.call-update) | async-done | bytes 98320 | tf_op jit(solution)/shard_map/psum | solution.py:27
  622.1 1.2 fusion.32
  623.3 79.5 %psum.59 = f32[32,32]{0,1:T(8,128)S(1)} all-reduce(f32[32,32]{0,1:T(8,128)S(1)} %fusion.32), channel_id=1, replica_groups=mesh['rows'=16,'params'=16] {'params'}, use_global_device_ids=true, to_apply=%region_8.11 | all-reduce | flops 1024 | bytes 8192 | tf_op jit(solution)/shard_map/psum | solution.py:28
  702.9 2.9 cholesky.85
  706.5 0.7 fusion.13
  707.1 2.5 custom-call.9
  709.6 1.2 fusion.1
  710.8 1.3 fusion.33
  712.2 77.8 %all-gather.13.cloned.1.call-done = f32[512,2048]{1,0:T(8,128)} async-done(((f32[32,2048]{1,0:T(8,128)}), f32[512,2048]{1,0:T(8,128)}) %all-gather.13.cloned.1.call-update) | async-done | bytes 4194320 | tf_op jit(solution)/shard_map/all_gather | solution.py:24
  790.0 2.4 reduce_sum.48
  792.4 1.7 fusion.6
  794.2 170.9 %all-reduce.9.cloned.1.call-done = f32[32,768]{1,0:T(8,128)} async-done(((f32[32,768]{1,0:T(8,128)}), f32[32,768]{1,0:T(8,128)}) %all-reduce.9.cloned.1.call-update) | async-done | bytes 98320 | tf_op jit(solution)/shard_map/psum | solution.py:27
  965.1 1.2 fusion.34
  966.3 79.5 %psum.61 = f32[32,32]{0,1:T(8,128)S(1)} all-reduce(f32[32,32]{0,1:T(8,128)S(1)} %fusion.34), channel_id=1, replica_groups=mesh['rows'=16,'params'=16] {'params'}, use_global_device_ids=true, to_apply=%region_11.14 | all-reduce | flops 1024 | bytes 8192 | tf_op jit(solution)/shard_map/psum | solution.py:28
  1045.9 2.9 cholesky.96
  1049.5 0.7 fusion.14
  1050.2 2.5 custom-call.10
  1052.6 1.2 fusion.2
  1053.8 1.3 fusion.35
  1055.2 77.8 %all-gather.15.cloned.1.call-done = f32[512,2048]{1,0:T(8,128)} async-done(((f32[32,2048]{1,0:T(8,128)}), f32[512,2048]{1,0:T(8,128)}) %all-gather.15.cloned.1.call-update) | async-done | bytes 4194320 | tf_op jit(solution)/shard_map/all_gather | solution.py:24
  1133.0 2.4 reduce_sum.49
  1135.5 1.7 fusion.7
  1137.2 171.0 %all-reduce.11.cloned.1.call-done = f32[32,768]{1,0:T(8,128)} async-done(((f32[32,768]{1,0:T(8,128)}), f32[32,768]{1,0:T(8,128)}) %all-reduce.11.cloned.1.call-update) | async-done | bytes 98320 | tf_op jit(solution)/shard_map/psum | solution.py:27
  1308.1 1.2 fusion.36
  1309.3 79.5 %psum.63 = f32[32,32]{0,1:T(8,128)S(1)} all-reduce(f32[32,32]{0,1:T(8,128)S(1)} %fusion.36), channel_id=1, replica_groups=mesh['rows'=16,'params'=16] {'params'}, use_global_device_ids=true, to_apply=%region_14.17 | all-reduce | flops 1024 | bytes 8192 | tf_op jit(solution)/shard_map/psum | solution.py:28
  1389.0 2.9 cholesky.107
  1391.9 0.6 compare_reduce_fusion
  1392.5 0.7 fusion.15
  1393.2 2.4 custom-call.11
  1395.6 1.8 fusion.3
  (40 shorter events, 3.0 us)
Async XLA Ops:
  6.5 7.7 copy-start
  6.5 97.4 %all-gather.9.cloned.1.call-start = ((), (), s32[]{:S(2)}) async-start(), calls=%async_computation.4 | async-start | bytes 4456448 | tf_op jit(solution)/shard_map/all_gather | solution.py:24
  14.2 1.4 copy-start.1
  14.2 1.4 copy-start.2
  15.6 263.4 %all-reduce.5.cloned.1.call-start = ((), (), s32[]{:S(2)}) async-start(), calls=%async_computation | async-start | bytes 196608 | tf_op jit(solution)/shard_map/psum | solution.py:27
  108.1 338.9 %all-gather.11.cloned.1.call-start = ((), (), s32[]{:S(2)}) async-start(), calls=%async_computation.5 | async-start | bytes 4456448 | tf_op jit(solution)/shard_map/all_gather | solution.py:24
  369.1 252.9 %all-reduce.7.cloned.1.call-start = ((), (), s32[]{:S(2)}) async-start(), calls=%async_computation.1 | async-start | bytes 196608 | tf_op jit(solution)/shard_map/psum | solution.py:27
  451.1 338.9 %all-gather.13.cloned.1.call-start = ((), (), s32[]{:S(2)}) async-start(), calls=%async_computation.6 | async-start | bytes 4456448 | tf_op jit(solution)/shard_map/all_gather | solution.py:24
  712.2 252.9 %all-reduce.9.cloned.1.call-start = ((), (), s32[]{:S(2)}) async-start(), calls=%async_computation.2 | async-start | bytes 196608 | tf_op jit(solution)/shard_map/psum | solution.py:27
  794.1 338.9 %all-gather.15.cloned.1.call-start = ((), (), s32[]{:S(2)}) async-start(), calls=%async_computation.7 | async-start | bytes 4456448 | tf_op jit(solution)/shard_map/all_gather | solution.py:24
  1055.2 252.9 %all-reduce.11.cloned.1.call-start = ((), (), s32[]{:S(2)}) async-start(), calls=%async_computation.3 | async-start | bytes 196608 | tf_op jit(solution)/shard_map/psum | solution.py:27
Sparse Core Ops, SparseCore 0:
  15.7 88.1 all-gather.8
  108.2 170.8 all-reduce.4
  369.2 77.6 all-gather.10
  451.2 170.8 all-reduce.6
  712.3 77.6 all-gather.12
  794.3 170.8 all-reduce.8
  1055.3 77.6 all-gather.14
  1137.3 170.8 all-reduce.10
